TPU v7x, 256 devices: a whole 4x4x8 slice. The times are simulated.
256 devices in a mesh: row: 8 (over x, core), col: 32 (over y, z).
Axes of the slice: x: 4, y: 4, z: 8, core: 2. Of those that a mesh axis runs over, the one named last changes fastest.
Arguments:
- hidden: bfloat16 [128, 8192], P('col', 'row'), may hold values from -6 to 6
- w_gate: bfloat16 [8192, 16384], P('row', 'col'), may hold values from -0.0625 to 0.0625
- w_up: bfloat16 [8192, 16384], P('row', 'col'), may hold values from -0.0625 to 0.0625
- prior: float32 [16384, 16384], P('row', 'col'), may hold values from -1 to 12, as said below
- rhs: float32 [16384, 4096], P('row', 'col'), may hold values from -6 to 6
Outputs:
- factored: float32 [16384, 16384], P('row', 'col')
- right_out: float32 [16384, 4096], P('row', 'col')
Inputs may be any that keep to these rules, and one draw needn't show every extreme that they name: prior is symmetric and positive definite, with smallest eigenvalue 0.1 or more.
All inputs are finite; a program needn't handle non-finite values.
Results may differ from a plain program's by a relative error of at most 0.0003.
Values may be sent and summed in bfloat16 or wider, within the bound.
No kernel may reach another device: no remote copies, remote signals or barrier semaphores. Data moves between devices by JAX's collectives and lax.ppermute only.
A program may use at most 64 MiB of HBM per device.

v0:
```python
import jax
import jax.numpy as jnp
from jax import lax
from jax.sharding import Mesh
from jax.sharding import PartitionSpec as P

P_SIZE = 128
PANELS = 2
COL = ("col_0", "col_1")
DAMP = 0.5


def joined_along(blocks, dim):
    blocks = jnp.moveaxis(blocks, 0, dim)
    lengths = blocks.shape
    return blocks.reshape(*lengths[:dim], lengths[dim] * lengths[dim + 1], *lengths[dim + 2 :])


def copy_for_each(shard, axis):
    peers = lax.axis_size(axis)
    return lax.all_to_all(
        jnp.broadcast_to(shard[None], (peers, *shard.shape)), axis, 0, 0, tiled=True
    )


def gathered_copies(shard, axis, dim):
    return joined_along(copy_for_each(shard, axis), dim)


def side_by_side(arrays, axis, dim, along):
    both = jnp.concatenate(arrays, axis=along)
    result, at, finished = (lax.psum_scatter(both, axis, scatter_dimension=dim, tiled=True), 0, [])
    for a in arrays:
        finished.append(lax.slice_in_dim(result, at, at + a.shape[along], axis=along))
        at += a.shape[along]
    return tuple(finished)


def spread(shard, axes, root):
    shard = jnp.where(lax.axis_index(axes) == root, shard, jnp.zeros_like(shard))
    for axis in axes:
        shard = lax.psum(shard, axis)
    return shard


def broadcast(shard, axis, root):
    return lax.dynamic_index_in_dim(lax.all_gather(shard, axis), root, 0, keepdims=False)


def local(hidden, w_gate, w_up, prior, rhs):
    rows_count = lax.axis_size("row")
    cols_count = lax.axis_size(COL)
    row_id = lax.axis_index("row")
    col_id = lax.axis_index(COL)
    ratio = cols_count // rows_count
    height, width = prior.shape
    tokens = gathered_copies(hidden, COL, 0)
    gate_part = jnp.dot(tokens, w_gate, preferred_element_type=jnp.float32)
    up_part = jnp.dot(tokens, w_up, preferred_element_type=jnp.float32)
    gate, upward = side_by_side((gate_part, up_part), "row", 0, 1)
    keys = gathered_copies(jax.nn.silu(gate) * upward, "row", 0)
    samples = keys.shape[0]
    regrouped = lax.all_to_all(keys, COL, split_axis=0, concat_axis=1, tiled=True)
    own_part = lax.dynamic_slice_in_dim(regrouped, row_id * height, height, 1)
    row_keys = gathered_copies(own_part, COL, 0)
    row_global = row_id * height + lax.iota(jnp.int32, height)
    col_global = col_id * width + lax.iota(jnp.int32, width)
    outer = lax.dot_general(
        row_keys,
        keys,
        (((0,), (0,)), ((), ())),
        precision=lax.Precision.HIGHEST,
        preferred_element_type=jnp.float32,
    )
    work = prior + outer / samples
    work = work + jnp.where(row_global[:, None] == col_global[None, :], DAMP, 0.0).astype(
        jnp.float32
    )
    right = rhs
    offsets = lax.iota(jnp.int32, P_SIZE)
    for panel in range(PANELS):
        start = panel * P_SIZE
        stop = start + P_SIZE
        column = spread(work[:, start:stop], COL, 0)
        pivot = jnp.linalg.cholesky(broadcast(column[start:stop], "row", 0))
        solved = jax.scipy.linalg.solve_triangular(pivot, column.T, lower=True).T
        placed = jnp.zeros_like(solved).at[start:stop].set(pivot)
        in_pivot = (row_global >= start) & (row_global < stop)
        beyond = row_global >= stop
        factor_cols = jnp.where(in_pivot[:, None], placed, jnp.where(beyond[:, None], solved, 0.0))
        matching = lax.dynamic_slice_in_dim(factor_cols, col_id % ratio * width, width, 0)
        across = broadcast(matching, "row", col_id // ratio)
        lower_rows = jnp.where(beyond[:, None], factor_cols, 0.0)
        upper_cols = jnp.where((col_global >= stop)[:, None], across, 0.0)
        work = work - lax.dot_general(
            lower_rows,
            upper_cols,
            (((1,), (1,)), ((), ())),
            precision=lax.Precision.HIGHEST,
            preferred_element_type=jnp.float32,
        )
        solution = jax.scipy.linalg.solve_triangular(
            factor_cols[start:stop], right[start:stop], lower=True
        )
        solution = broadcast(solution, "row", 0)
        right = right - jnp.dot(
            lower_rows,
            solution,
            precision=lax.Precision.HIGHEST,
            preferred_element_type=jnp.float32,
        )
        right = right.at[start:stop].set(jnp.where(row_id == 0, solution, right[start:stop]))
        keep_factor = (row_global[:, None] >= start + offsets[None, :]) & (col_id == 0)
        work = work.at[:, start:stop].set(jnp.where(keep_factor, factor_cols, work[:, start:stop]))
    return (work, right)


def solution(mesh):
    finer = Mesh(mesh.devices.reshape(mesh.shape["row"], 4, 8), ("row", "col_0", "col_1"))
    placed = (P(COL, "row"), P("row", COL), P("row", COL), P("row", COL), P("row", COL))
    return jax.shard_map(
        local,
        mesh=finer,
        in_specs=placed,
        out_specs=(P("row", COL), P("row", COL)),
        check_vma=False,
    )
```

profile of v0, /device:TPU:1, one launch (start us, length us, event | category | flops | bytes accessed | tf_op | source)
XLA Modules:
  0.0 588.0 jit_solution(16554936312668972503)
XLA Ops:
  8.1 21.5 %all_to_all.34 = bf16[32,4,1024]{2,1,0:T(4,128)(2,1)S(1)} all-to-all(bf16[32,4,1024]{2,1,0:T(4,128)(2,1)S(1)} %broadcast_in_dim.100), channel_id=1, replica_groups=mesh['row'=8,'col_0'=4,'col_1'=8] {'col_0','col_1'}, dimensions={0} | all-to-all | bytes 524288 | tf_op jit(solution)/shard_map/all_to_all | solution.py:21
  32.4 30.2 %reduce-scatter.2.cloned.1.call-done = f32[16,1024]{1,0:T(8,128)} async-done(((f32[128,1024]{1,0:T(8,128)}), f32[16,1024]{1,0:T(8,128)}) %reduce-scatter.2.cloned.1.call-update) | async-done | bytes 65552 | tf_op jit(solution)/shard_map/reduce_scatter | solution.py:32
  63.4 11.9 %all_to_all.35 = f32[8,16,512]{2,1,0:T(8,128)S(1)} all-to-all(f32[8,16,512]{2,1,0:T(8,128)S(1)} %broadcast_in_dim.101), channel_id=1, replica_groups=mesh['row'=8,'col_0'=4,'col_1'=8] {'row'}, dimensions={0} | all-to-all | bytes 524288 | tf_op jit(solution)/shard_map/all_to_all | solution.py:21
  76.0 9.6 %all-to-all-start.2 = ((f32[32,4,512]{2,1,0:T(4,128)}), f32[32,4,512]{2,1,0:T(4,128)S(1)}, u32[]{:S(2)}, u32[]{:S(2)}) async-start(f32[32,4,512]{2,1,0:T(4,128)} %all_to_all.25), calls=%async_computation.3 | async-start | bytes 524288 | tf_op jit(solution)/shard_map/all_to_all | solution.py:63
  85.6 9.7 %all-to-all-done.2 = f32[32,4,512]{2,1,0:T(4,128)S(1)} async-done(((f32[32,4,512]{2,1,0:T(4,128)}), f32[32,4,512]{2,1,0:T(4,128)S(1)}, u32[]{:S(2)}, u32[]{:S(2)}) %all-to-all-start.2) | async-done | bytes 262176 | tf_op jit(solution)/shard_map/all_to_all | solution.py:63
  96.5 6.0 %all-to-all-start.3 = ((f32[32,4,2048]{2,1,0:T(4,128)}), f32[32,4,2048]{2,1,0:T(4,128)S(1)}, u32[]{:S(2)}, u32[]{:S(2)}) async-start(f32[32,4,2048]{2,1,0:T(4,128)} %broadcast_in_dim.102), calls=%async_computation.4 | async-start | bytes 2097152 | tf_op jit(solution)/shard_map/all_to_all | solution.py:21
  102.6 24.3 %all-to-all-done.3 = f32[32,4,2048]{2,1,0:T(4,128)S(1)} async-done(((f32[32,4,2048]{2,1,0:T(4,128)}), f32[32,4,2048]{2,1,0:T(4,128)S(1)}, u32[]{:S(2)}, u32[]{:S(2)}) %all-to-all-start.3) | async-done | bytes 1048608 | tf_op jit(solution)/shard_map/all_to_all | solution.py:21
  127.3 5.8 select_add_fusion
  136.3 48.9 %all-reduce.7.cloned.1.call-done = f32[2048,128]{1,0:T(8,128)} async-done(((f32[2048,128]{1,0:T(8,128)}), f32[2048,128]{1,0:T(8,128)}) %all-reduce.7.cloned.1.call-update) | async-done | bytes 1048592 | tf_op jit(solution)/shard_map/psum | solution.py:42
  185.3 76.3 %all-reduce.9.cloned.1.call-done = f32[2048,128]{1,0:T(8,128)} async-done(((f32[2048,128]{1,0:T(8,128)}), f32[2048,128]{1,0:T(8,128)}) %all-reduce.9.cloned.1.call-update) | async-done | bytes 1048592 | tf_op jit(solution)/shard_map/psum | solution.py:42
  262.5 18.2 %all-gather = f32[1024,128]{1,0:T(8,128)S(1)} all-gather(f32[128,128]{1,0:T(8,128)S(1)} %slice.179), channel_id=2, replica_groups=mesh['row'=8,'col_0'=4,'col_1'=8] {'row'}, dimensions={0}, use_global_device_ids=true | all-gather | bytes 589824 | tf_op jit(solution)/shard_map/all_gather | solution.py:47
  280.9 11.7 %cholesky.44 = f32[128,128]{1,0:T(8,128)S(1)} custom-call(f32[128,128]{1,0:T(8,128)S(1)} %copy.8), custom_call_target="Cholesky" | custom-call | tf_op jit(solution)/shard_map/jit(cholesky)/cholesky | solution.py:85
  294.0 9.8 %custom-call.10 = f32[1,128,128]{1,2,0:T(8,128)S(1)} custom-call(f32[1,128,128]{2,1,0:T(8,128)S(1)} %get-tuple-element.79), custom_call_target="InvertDiagBlocksLowerTriangular" | custom-call | tf_op jit(solution)/shard_map/jit(_solve_triangular)/triangular_solve | solution.py:86
  308.5 24.7 %all-gather.9.cloned.1.call-done = f32[4096,128]{1,0:T(8,128)} async-done(((f32[512,128]{1,0:T(8,128)}), f32[4096,128]{1,0:T(8,128)}) %all-gather.9.cloned.1.call-update) | async-done | bytes 2097168 | tf_op jit(solution)/shard_map/all_gather | solution.py:47
  343.1 49.5 %all-reduce.11.cloned.1.call-done = f32[2048,128]{1,0:T(8,128)} async-done(((f32[2048,128]{1,0:T(8,128)}), f32[2048,128]{1,0:T(8,128)}) %all-reduce.11.cloned.1.call-update) | async-done | bytes 1048592 | tf_op jit(solution)/shard_map/psum | solution.py:42
  392.7 76.3 %all-reduce.13.cloned.1.call-done = f32[2048,128]{1,0:T(8,128)} async-done(((f32[2048,128]{1,0:T(8,128)}), f32[2048,128]{1,0:T(8,128)}) %all-reduce.13.cloned.1.call-update) | async-done | bytes 1048592 | tf_op jit(solution)/shard_map/psum | solution.py:42
  469.9 18.3 %all-gather.2 = f32[1024,128]{1,0:T(8,128)S(1)} all-gather(f32[128,128]{1,0:T(8,128)S(1)} %slice.183), channel_id=4, replica_groups=mesh['row'=8,'col_0'=4,'col_1'=8] {'row'}, dimensions={0}, use_global_device_ids=true | all-gather | bytes 589824 | tf_op jit(solution)/shard_map/all_gather | solution.py:47
  488.3 11.7 %cholesky.55 = f32[128,128]{1,0:T(8,128)S(1)} custom-call(f32[128,128]{1,0:T(8,128)S(1)} %copy.11), custom_call_target="Cholesky" | custom-call | tf_op jit(solution)/shard_map/jit(cholesky)/cholesky | solution.py:85
  501.4 9.8 %custom-call.11 = f32[1,128,128]{1,2,0:T(8,128)S(1)} custom-call(f32[1,128,128]{2,1,0:T(8,128)S(1)} %get-tuple-element.77), custom_call_target="InvertDiagBlocksLowerTriangular" | custom-call | tf_op jit(solution)/shard_map/jit(_solve_triangular)/triangular_solve | solution.py:86
  515.9 9.8 %custom-call.12 = f32[1,128,128]{1,2,0:T(8,128)S(1)} custom-call(f32[1,128,128]{2,1,0:T(8,128)S(1)} %fusion.32), custom_call_target="InvertDiagBlocksLowerTriangular" | custom-call | tf_op jit(solution)/shard_map/jit(_solve_triangular)/triangular_solve | solution.py:102
  526.9 14.2 %all-gather.4 = f32[1024,128]{1,0:T(8,128)S(1)} all-gather(f32[128,128]{1,0:T(8,128)S(1)} %fusion.34), channel_id=6, replica_groups=mesh['row'=8,'col_0'=4,'col_1'=8] {'row'}, dimensions={0}, use_global_device_ids=true | all-gather | bytes 589824 | tf_op jit(solution)/shard_map/all_gather | solution.py:47
  545.7 9.8 %custom-call.13 = f32[1,128,128]{1,2,0:T(8,128)S(1)} custom-call(f32[1,128,128]{2,1,0:T(8,128)S(1)} %fusion.30), custom_call_target="InvertDiagBlocksLowerTriangular" | custom-call | tf_op jit(solution)/shard_map/jit(_solve_triangular)/triangular_solve | solution.py:102
  556.6 13.1 %all-gather.5 = f32[1024,128]{1,0:T(8,128)S(1)} all-gather(f32[128,128]{1,0:T(8,128)S(1)} %fusion.28), channel_id=7, replica_groups=mesh['row'=8,'col_0'=4,'col_1'=8] {'row'}, dimensions={0}, use_global_device_ids=true | all-gather | bytes 589824 | tf_op jit(solution)/shard_map/all_gather | solution.py:47
  572.1 5.9 %convolution_subtract_fusion = f32[2048,512]{1,0:T(8,128)S(1)} fusion(f32[2048,512]{1,0:T(8,128)} %copy-done.1, f32[2048,128]{1,0:T(8,128)S(1)} %fusion.1, pred[2048]{0:T(1024)(128)(4,1)S(1)} %fusion.44, f32[8,512,128]{2,1,0:T(8,128)} %bitcast.62, s32[]{:T(128)S(6)} %select_n.113, pred[512]{0:T(512)(128)(4,1)S(1)} %fusion.52), kind=kOutput, calls=%fused_computation.1 | convolution fusion | flops 1611988992 | bytes 9701892 | tf_op jit(solution)/shard_map/dot_general | solution.py:95
  (79 shorter events, 46.3 us)
Async XLA Ops:
  7.2 22.5 %copy-start = (bf16[1024,512]{1,0:T(8,128)(2,1)S(1)}, bf16[1024,512]{1,0:T(8,128)(2,1)}, u32[]{:S(2)}) copy-start(bf16[1024,512]{1,0:T(8,128)(2,1)} %param.23) | copy-start | bytes 3145732
  7.2 55.4 %reduce-scatter.2.cloned.1.call-start = ((), (), s32[]{:S(2)}) async-start(), calls=%async_computation.5 | async-start | bytes 589824 | tf_op jit(solution)/shard_map/reduce_scatter | solution.py:32
  76.0 19.2 %all-to-all-start.2 = ((f32[32,4,512]{2,1,0:T(4,128)}), f32[32,4,512]{2,1,0:T(4,128)S(1)}, u32[]{:S(2)}, u32[]{:S(2)}) async-start(f32[32,4,512]{2,1,0:T(4,128)} %all_to_all.25), calls=%async_computation.3 | async-start | bytes 524288 | tf_op jit(solution)/shard_map/all_to_all | solution.py:63
  96.5 30.5 %all-to-all-start.3 = ((f32[32,4,2048]{2,1,0:T(4,128)}), f32[32,4,2048]{2,1,0:T(4,128)S(1)}, u32[]{:S(2)}, u32[]{:S(2)}) async-start(f32[32,4,2048]{2,1,0:T(4,128)} %broadcast_in_dim.102), calls=%async_computation.4 | async-start | bytes 2097152 | tf_op jit(solution)/shard_map/all_to_all | solution.py:21
  102.6 82.6 %all-reduce.7.cloned.1.call-start = ((), (), s32[]{:S(2)}) async-start(), calls=%async_computation.6 | async-start | bytes 2097152 | tf_op jit(solution)/shard_map/psum | solution.py:42
  133.1 2.0 copy-start.2
  136.3 125.4 %all-reduce.9.cloned.1.call-start = ((), (), s32[]{:S(2)}) async-start(), calls=%async_computation.7 | async-start | bytes 2097152 | tf_op jit(solution)/shard_map/psum | solution.py:42
  185.2 148.1 %all-gather.9.cloned.1.call-start = ((), (), s32[]{:S(2)}) async-start(), calls=%async_computation.10 | async-start | bytes 2359296 | tf_op jit(solution)/shard_map/all_gather | solution.py:47
  307.8 84.8 %all-reduce.11.cloned.1.call-start = ((), (), s32[]{:S(2)}) async-start(), calls=%async_computation.8 | async-start | bytes 2097152 | tf_op jit(solution)/shard_map/psum | solution.py:42
  339.9 2.0 copy-start.1
  343.0 126.0 %all-reduce.13.cloned.1.call-start = ((), (), s32[]{:S(2)}) async-start(), calls=%async_computation.9 | async-start | bytes 2097152 | tf_op jit(solution)/shard_map/psum | solution.py:42
  392.6 179.5 %all-gather.11.cloned.1.call-start = ((), (), s32[]{:S(2)}) async-start(), calls=%async_computation.11 | async-start | bytes 2359296 | tf_op jit(solution)/shard_map/all_gather | solution.py:47
  572.1 5.9 %copy-start.4 = (f32[2048,128]{1,0:T(8,128)}, f32[2048,128]{1,0:T(8,128)S(1)}, u32[]{:S(2)}) copy-start(f32[2048,128]{1,0:T(8,128)S(1)} %fusion.27) | copy-start | bytes 3145732
  579.1 2.0 copy-start.3
Sparse Core Ops, SparseCore 0:
  32.5 29.9 reduce-scatter.1
  136.4 48.7 all-reduce.6
  187.5 74.0 all-reduce.8
  307.9 25.3 all-gather.8
  343.1 49.4 all-reduce.10
  394.9 74.0 all-reduce.12
  515.4 26.1 all-gather.10
where the time goes:
time: 589 us; the launch traced here: 588 us
  waiting for transfers between devices  340 us (58%)
  blocking collectives  97.3 us (17%)
  other arithmetic  74.2 us (13%)
  matrix products  33.2 us (6%)
  starting transfers between devices  15.9 us (3%)
  between operations  14.5 us (2%)
  local copies, waits for them, and re-layouts  12.9 us (2%)
    psum x4, waiting for transfers between devices, spread(): shard = lax.psum(shard, axis)  251 us
    all_gather x4, blocking collectives, broadcast(): lax.all_gather(shard, axis)  63.8 us
    all_to_all x2, blocking collectives, copy_for_each(): lax.all_to_all(jnp.broadcast_to(shard[None], (peers, *shard.shape)), axis...  33.4 us
    reduce_scatter x1, waiting for transfers between devices, side_by_side(): lax.psum_scatter(both, axis, scatter_dimension=dim, tiled=True)  30.2 us
    another operation x6, other arithmetic, local(): pivot = jnp.linalg.cholesky(broadcast(column[start:stop], 'row', 0))  24.8 us
    all_gather x2, waiting for transfers between devices, broadcast(): lax.all_gather(shard, axis)  24.7 us
    all_to_all x1, waiting for transfers between devices, copy_for_each(): lax.all_to_all(jnp.broadcast_to(shard[None], (peers, *shard.shape)), axis...  24.3 us
    another operation x4, other arithmetic, local(): solved = jax.scipy.linalg.solve_triangular(pivot, column.T, lower=True).T  20.9 us
  transfers between devices with their start and end apart: 9, of which 8 were waited for; matrix products, arithmetic and copies ran while one was open for 5% of the time, Pallas kernels for 0%

commit v1 on v0

--- a/solution.py
+++ b/solution.py
@@ -39,7 +39,12 @@
 def spread(shard, axes, root):
     shard = jnp.where(lax.axis_index(axes) == root, shard, jnp.zeros_like(shard))
     for axis in axes:
-        shard = lax.psum(shard, axis)
+
+        def _note_knots(x_local, mesh_ax):
+            mid_arr = jnp.sum(lax.all_gather(x_local, mesh_ax), axis=0)
+            return mid_arr
+
+        shard = _note_knots(shard, axis)
     return shard
 
 

time: 589 us -> 626 us (1.063)
  waiting for transfers between devices: 340 us -> 380 us
  other arithmetic: 74.2 us -> 89 us
  blocking collectives: 97.3 us -> 88.9 us
  matrix products: 33.2 us -> 26.5 us
    all_gather x0 -> x4, waiting for transfers between devices: none -> 290 us  [_note_knots(): mid_arr = jnp.sum(lax.all_gather(x_local, mesh_ax), axis=0)]
    psum x4 -> x0, waiting for transfers between devices: 251 us -> none  [spread(): shard = lax.psum(shard, axis)]
    reduce_sum x0 -> x4, other arithmetic: none -> 14.8 us  [_note_knots(): mid_arr = jnp.sum(lax.all_gather(x_local, mesh_ax), axis=0)]
    all_gather x4, blocking collectives: 63.8 us -> 55.5 us  [broadcast(): lax.all_gather(shard, axis)]
where the time goes in v1:
time: 626 us
  waiting for transfers between devices  380 us (61%)
  other arithmetic  89 us (14%)
  blocking collectives  88.9 us (14%)
  matrix products  26.5 us (4%)
  starting transfers between devices  15.8 us (3%)
  between operations  14.5 us (2%)
  local copies, waits for them, and re-layouts  11.2 us (2%)
    all_gather x4, waiting for transfers between devices, _note_knots(): mid_arr = jnp.sum(lax.all_gather(x_local, mesh_ax), axis=0)  290 us
    all_gather x4, blocking collectives, broadcast(): lax.all_gather(shard, axis)  55.5 us
    all_to_all x2, blocking collectives, copy_for_each(): lax.all_to_all(jnp.broadcast_to(shard[None], (peers, *shard.shape)), axis...  33.4 us
    reduce_scatter x1, waiting for transfers between devices, side_by_side(): lax.psum_scatter(both, axis, scatter_dimension=dim, tiled=True)  30.2 us
    all_gather x2, waiting for transfers between devices, broadcast(): lax.all_gather(shard, axis)  25 us
    another operation x6, other arithmetic, local(): pivot = jnp.linalg.cholesky(broadcast(column[start:stop], 'row', 0))  24.8 us
    all_to_all x1, waiting for transfers between devices, copy_for_each(): lax.all_to_all(jnp.broadcast_to(shard[None], (peers, *shard.shape)), axis...  24.3 us
    another operation x4, other arithmetic, local(): solved = jax.scipy.linalg.solve_triangular(pivot, column.T, lower=True).T  20.9 us
  transfers between devices with their start and end apart: 9, of which 8 were waited for; matrix products, arithmetic and copies ran while one was open for 5% of the time, Pallas kernels for 0%

profile of v1, /device:TPU:1, one launch (start us, length us, event | category | flops | bytes accessed | tf_op | source)
XLA Modules:
  0.0 625.5 jit_solution(7888110909538426722)
XLA Ops:
  8.1 21.5 %all_to_all.34 = bf16[32,4,1024]{2,1,0:T(4,128)(2,1)S(1)} all-to-all(bf16[32,4,1024]{2,1,0:T(4,128)(2,1)S(1)} %broadcast_in_dim.100), channel_id=1, replica_groups=mesh['row'=8,'col_0'=4,'col_1'=8] {'col_0','col_1'}, dimensions={0} | all-to-all | bytes 524288 | tf_op jit(solution)/shard_map/all_to_all | solution.py:21
  32.4 30.2 %reduce-scatter.2.cloned.1.call-done = f32[16,1024]{1,0:T(8,128)} async-done(((f32[128,1024]{1,0:T(8,128)}), f32[16,1024]{1,0:T(8,128)}) %reduce-scatter.2.cloned.1.call-update) | async-done | bytes 65552 | tf_op jit(solution)/shard_map/reduce_scatter | solution.py:32
  63.5 11.9 %all_to_all.35 = f32[8,16,512]{2,1,0:T(8,128)S(1)} all-to-all(f32[8,16,512]{2,1,0:T(8,128)S(1)} %broadcast_in_dim.101), channel_id=1, replica_groups=mesh['row'=8,'col_0'=4,'col_1'=8] {'row'}, dimensions={0} | all-to-all | bytes 524288 | tf_op jit(solution)/shard_map/all_to_all | solution.py:21
  76.1 9.5 %all-to-all-start.2 = ((f32[32,4,512]{2,1,0:T(4,128)}), f32[32,4,512]{2,1,0:T(4,128)S(1)}, u32[]{:S(2)}, u32[]{:S(2)}) async-start(f32[32,4,512]{2,1,0:T(4,128)} %all_to_all.25), calls=%async_computation.3 | async-start | bytes 524288 | tf_op jit(solution)/shard_map/all_to_all | solution.py:68
  85.6 9.7 %all-to-all-done.2 = f32[32,4,512]{2,1,0:T(4,128)S(1)} async-done(((f32[32,4,512]{2,1,0:T(4,128)}), f32[32,4,512]{2,1,0:T(4,128)S(1)}, u32[]{:S(2)}, u32[]{:S(2)}) %all-to-all-start.2) | async-done | bytes 262176 | tf_op jit(solution)/shard_map/all_to_all | solution.py:68
  96.5 6.0 all-to-all-start.3
  102.6 24.3 %all-to-all-done.3 = f32[32,4,2048]{2,1,0:T(4,128)S(1)} async-done(((f32[32,4,2048]{2,1,0:T(4,128)}), f32[32,4,2048]{2,1,0:T(4,128)S(1)}, u32[]{:S(2)}, u32[]{:S(2)}) %all-to-all-start.3) | async-done | bytes 1048608 | tf_op jit(solution)/shard_map/all_to_all | solution.py:21
  127.3 5.8 select_add_fusion
  136.3 50.2 %all-gather.17.cloned.1.call-done = f32[8192,128]{1,0:T(8,128)} async-done(((f32[2048,128]{1,0:T(8,128)}), f32[8192,128]{1,0:T(8,128)}) %all-gather.17.cloned.1.call-update) | async-done | bytes 4194320 | tf_op jit(solution)/shard_map/all_gather | solution.py:44
  190.1 94.6 %all-gather.19.cloned.1.call-done = f32[16384,128]{1,0:T(8,128)} async-done(((f32[2048,128]{1,0:T(8,128)}), f32[16384,128]{1,0:T(8,128)}) %all-gather.19.cloned.1.call-update) | async-done | bytes 8388624 | tf_op jit(solution)/shard_map/all_gather | solution.py:44
  288.6 14.1 %all-gather.2 = f32[1024,128]{0,1:T(8,128)S(1)} all-gather(f32[128,128]{0,1:T(8,128)S(1)} %copy.19), channel_id=4, replica_groups=mesh['row'=8,'col_0'=4,'col_1'=8] {'row'}, dimensions={0}, use_global_device_ids=true | all-gather | bytes 589824 | tf_op jit(solution)/shard_map/all_gather | solution.py:52
  302.9 11.7 %cholesky.44 = f32[128,128]{1,0:T(8,128)S(1)} custom-call(f32[128,128]{1,0:T(8,128)S(1)} %fusion.39), custom_call_target="Cholesky" | custom-call | tf_op jit(solution)/shard_map/jit(cholesky)/cholesky | solution.py:90
  315.9 9.8 %custom-call.10 = f32[1,128,128]{1,2,0:T(8,128)S(1)} custom-call(f32[1,128,128]{2,1,0:T(8,128)S(1)} %get-tuple-element.79), custom_call_target="InvertDiagBlocksLowerTriangular" | custom-call | tf_op jit(solution)/shard_map/jit(_solve_triangular)/triangular_solve | solution.py:91
  328.3 25.0 %all-gather.21.cloned.1.call-done = f32[4096,128]{1,0:T(8,128)} async-done(((f32[512,128]{1,0:T(8,128)}), f32[4096,128]{1,0:T(8,128)}) %all-gather.21.cloned.1.call-update) | async-done | bytes 2097168 | tf_op jit(solution)/shard_map/all_gather | solution.py:52
  363.1 50.9 %all-gather.23.cloned.1.call-done = f32[8192,128]{1,0:T(8,128)} async-done(((f32[2048,128]{1,0:T(8,128)}), f32[8192,128]{1,0:T(8,128)}) %all-gather.23.cloned.1.call-update) | async-done | bytes 4194320 | tf_op jit(solution)/shard_map/all_gather | solution.py:44
  417.6 94.6 %all-gather.25.cloned.1.call-done = f32[16384,128]{1,0:T(8,128)} async-done(((f32[2048,128]{1,0:T(8,128)}), f32[16384,128]{1,0:T(8,128)}) %all-gather.25.cloned.1.call-update) | async-done | bytes 8388624 | tf_op jit(solution)/shard_map/all_gather | solution.py:44
  516.1 14.1 %all-gather.6 = f32[1024,128]{0,1:T(8,128)S(1)} all-gather(f32[128,128]{0,1:T(8,128)S(1)} %copy.20), channel_id=8, replica_groups=mesh['row'=8,'col_0'=4,'col_1'=8] {'row'}, dimensions={0}, use_global_device_ids=true | all-gather | bytes 589824 | tf_op jit(solution)/shard_map/all_gather | solution.py:52
  530.4 11.7 %cholesky.55 = f32[128,128]{1,0:T(8,128)S(1)} custom-call(f32[128,128]{1,0:T(8,128)S(1)} %fusion.37), custom_call_target="Cholesky" | custom-call | tf_op jit(solution)/shard_map/jit(cholesky)/cholesky | solution.py:90
  543.5 9.8 %custom-call.11 = f32[1,128,128]{1,2,0:T(8,128)S(1)} custom-call(f32[1,128,128]{2,1,0:T(8,128)S(1)} %get-tuple-element.77), custom_call_target="InvertDiagBlocksLowerTriangular" | custom-call | tf_op jit(solution)/shard_map/jit(_solve_triangular)/triangular_solve | solution.py:91
  555.8 9.8 %custom-call.12 = f32[1,128,128]{1,2,0:T(8,128)S(1)} custom-call(f32[1,128,128]{2,1,0:T(8,128)S(1)} %fusion.32), custom_call_target="InvertDiagBlocksLowerTriangular" | custom-call | tf_op jit(solution)/shard_map/jit(_solve_triangular)/triangular_solve | solution.py:107
  566.7 14.1 %all-gather.8 = f32[1024,128]{1,0:T(8,128)S(1)} all-gather(f32[128,128]{1,0:T(8,128)S(1)} %fusion.34), channel_id=10, replica_groups=mesh['row'=8,'col_0'=4,'col_1'=8] {'row'}, dimensions={0}, use_global_device_ids=true | all-gather | bytes 589824 | tf_op jit(solution)/shard_map/all_gather | solution.py:52
  583.2 9.8 %custom-call.13 = f32[1,128,128]{1,2,0:T(8,128)S(1)} custom-call(f32[1,128,128]{2,1,0:T(8,128)S(1)} %fusion.30), custom_call_target="InvertDiagBlocksLowerTriangular" | custom-call | tf_op jit(solution)/shard_map/jit(_solve_triangular)/triangular_solve | solution.py:107
  593.3 13.1 %all-gather.9 = f32[1024,128]{1,0:T(8,128)S(1)} all-gather(f32[128,128]{1,0:T(8,128)S(1)} %fusion.28), channel_id=11, replica_groups=mesh['row'=8,'col_0'=4,'col_1'=8] {'row'}, dimensions={0}, use_global_device_ids=true | all-gather | bytes 589824 | tf_op jit(solution)/shard_map/all_gather | solution.py:52
  610.0 5.6 convolution_subtract_fusion
  (83 shorter events, 53.1 us)
Async XLA Ops:
  7.2 22.5 %copy-start = (bf16[1024,512]{1,0:T(8,128)(2,1)S(1)}, bf16[1024,512]{1,0:T(8,128)(2,1)}, u32[]{:S(2)}) copy-start(bf16[1024,512]{1,0:T(8,128)(2,1)} %param.23) | copy-start | bytes 3145732
  7.2 55.5 %reduce-scatter.2.cloned.1.call-start = ((), (), s32[]{:S(2)}) async-start(), calls=%async_computation.5 | async-start | bytes 589824 | tf_op jit(solution)/shard_map/reduce_scatter | solution.py:32
  76.1 19.2 %all-to-all-start.2 = ((f32[32,4,512]{2,1,0:T(4,128)}), f32[32,4,512]{2,1,0:T(4,128)S(1)}, u32[]{:S(2)}, u32[]{:S(2)}) async-start(f32[32,4,512]{2,1,0:T(4,128)} %all_to_all.25), calls=%async_computation.3 | async-start | bytes 524288 | tf_op jit(solution)/shard_map/all_to_all | solution.py:68
  96.5 30.5 %all-to-all-start.3 = ((f32[32,4,2048]{2,1,0:T(4,128)}), f32[32,4,2048]{2,1,0:T(4,128)S(1)}, u32[]{:S(2)}, u32[]{:S(2)}) async-start(f32[32,4,2048]{2,1,0:T(4,128)} %broadcast_in_dim.102), calls=%async_computation.4 | async-start | bytes 2097152 | tf_op jit(solution)/shard_map/all_to_all | solution.py:21
  102.6 83.9 %all-gather.17.cloned.1.call-start = ((), (), s32[]{:S(2)}) async-start(), calls=%async_computation.6 | async-start | bytes 5242880 | tf_op jit(solution)/shard_map/all_gather | solution.py:44
  133.1 2.0 copy-start.3
  136.3 148.4 %all-gather.19.cloned.1.call-start = ((), (), s32[]{:S(2)}) async-start(), calls=%async_computation.7 | async-start | bytes 9437184 | tf_op jit(solution)/shard_map/all_gather | solution.py:44
  190.0 163.3 %all-gather.21.cloned.1.call-start = ((), (), s32[]{:S(2)}) async-start(), calls=%async_computation.8 | async-start | bytes 2359296 | tf_op jit(solution)/shard_map/all_gather | solution.py:52
  327.5 86.5 %all-gather.23.cloned.1.call-start = ((), (), s32[]{:S(2)}) async-start(), calls=%async_computation.9 | async-start | bytes 5242880 | tf_op jit(solution)/shard_map/all_gather | solution.py:44
  359.9 2.0 copy-start.2
  363.0 149.1 %all-gather.25.cloned.1.call-start = ((), (), s32[]{:S(2)}) async-start(), calls=%async_computation.10 | async-start | bytes 9437184 | tf_op jit(solution)/shard_map/all_gather | solution.py:44
  417.5 192.5 %all-gather.27.cloned.1.call-start = ((), (), s32[]{:S(2)}) async-start(), calls=%async_computation.11 | async-start | bytes 2359296 | tf_op jit(solution)/shard_map/all_gather | solution.py:52
  610.0 8.7 %copy-start.1 = (bf16[1024,512]{1,0:T(8,128)(2,1)S(1)}, bf16[1024,512]{1,0:T(8,128)(2,1)}, u32[]{:S(2)}) copy-start(bf16[1024,512]{1,0:T(8,128)(2,1)} %param.23) | copy-start | bytes 3145732
  616.7 2.0 copy-start.4
Sparse Core Ops, SparseCore 0:
  32.5 30.0 reduce-scatter.1
  136.4 50.0 all-gather.16
  190.1 94.4 all-gather.18
  327.6 25.6 all-gather.20
  363.2 50.7 all-gather.22
  417.6 94.4 all-gather.24
  555.2 26.3 all-gather.26
